TPU v7x, 512 devices: a whole 4x8x8 slice. The times are simulated.
512 devices in a mesh: row: 16 (over y_lo, x, core), col: 8 (over z), seq: 4 (over y_hi).
Axes of the slice: x: 4, y: 8 (y_hi: 4, y_lo: 2; y = y_hi * 2 + y_lo), z: 8, core: 2. Of those that a mesh axis runs over, the one named last changes fastest.
Arguments:
- left_piece: bfloat16 [512, 32, 1024], P('seq', None, 'row'), may hold values from -6 to 6
- right_piece: bfloat16 [512, 32, 1024], P('seq', 'row', 'col'), may hold values from -6 to 6
- proj_weight: bfloat16 [1024, 128], replicated, may hold values from -4 to 4
- proj_bias: float32 [128], replicated, may hold values from -3 to 3
- pair_rep: bfloat16 [1024, 1024, 128], P(('row', 'seq'), 'col'), may hold values from -6 to 6
- norm_gain: float32 [128], replicated, may hold values from 0.5 to 1.5
- up_weight: bfloat16 [128, 512], replicated, may hold values from -0.5 to 0.5
- up_bias: float32 [512], replicated, may hold values from -3 to 3
- down_weight: bfloat16 [512, 128], replicated, may hold values from -0.25 to 0.25
- down_bias: float32 [128], replicated, may hold values from -3 to 3
Outputs:
- refined: bfloat16 [1024, 1024, 128], P(('row', 'seq'), 'col')
All inputs are finite; a program needn't handle non-finite values.
Results may differ from a plain program's by a relative error of at most 0.0085.
Values may be sent and summed in bfloat16 or wider, within the bound.
A program may use at most 64 MiB of HBM per device.

v0:
```python
import jax
import jax.numpy as jnp
from jax import lax
from jax.sharding import PartitionSpec as P

epsilon = 1e-05


def project_block(row_slab, right_all, proj_weight):
    seq_count, channels, row_count = row_slab.shape
    columns = right_all.shape[2]
    left_mat = row_slab.reshape(seq_count, channels * row_count)
    right_mat = right_all.reshape(seq_count, channels * columns)
    outer_prod = lax.dot_general(
        left_mat, right_mat, (((0,), (0,)), ((), ())), preferred_element_type=jnp.float32
    ).astype(jnp.bfloat16)
    outer_prod = outer_prod.reshape(channels, row_count, channels, columns).transpose(1, 3, 0, 2)
    outer_prod = outer_prod.reshape(row_count * columns, channels * channels)
    result = jnp.dot(outer_prod, proj_weight, preferred_element_type=jnp.float32)
    return result.reshape(row_count, columns, proj_weight.shape[1])


def project_rows(row_slab, right_all, proj_weight):
    seq_count, channels, row_count = row_slab.shape
    sub_rows = 8
    pieces = row_slab.reshape(seq_count, channels, row_count // sub_rows, sub_rows)
    pieces = jnp.moveaxis(pieces, 2, 0)
    result = lax.map(lambda portion: project_block(portion, right_all, proj_weight), pieces)
    return result.reshape(row_count, right_all.shape[2], proj_weight.shape[1])


def transition(middle, norm_gain, up_weight, up_bias, down_weight, down_bias):
    row_count, columns, channels = middle.shape
    values = middle.astype(jnp.float32).reshape(row_count * columns, channels)
    center = jnp.mean(values, axis=1, keepdims=True)
    spread = jnp.mean(jnp.square(values - center), axis=1, keepdims=True)
    normed = ((values - center) * lax.rsqrt(spread + epsilon) * norm_gain).astype(jnp.bfloat16)
    hidden = jnp.maximum(
        jnp.dot(normed, up_weight, preferred_element_type=jnp.float32) + up_bias, 0.0
    ).astype(jnp.bfloat16)
    result = values + jnp.dot(hidden, down_weight, preferred_element_type=jnp.float32) + down_bias
    return result.astype(jnp.bfloat16).reshape(row_count, columns, channels)


def gather_right(right_part):
    return lax.all_gather(right_part, "row", axis=1, tiled=True)


def move_cols(tile):
    return lax.all_to_all(tile, "col", split_axis=0, concat_axis=2, tiled=True)


def on_device(
    left_piece,
    right_piece,
    proj_weight,
    proj_bias,
    pair_rep,
    norm_gain,
    up_weight,
    up_bias,
    down_weight,
    down_bias,
):
    own_rows = pair_rep.shape[0]
    columns = pair_rep.shape[1]
    channels = pair_rep.shape[2]
    groups = lax.axis_size("seq")
    seq_index = lax.axis_index("seq")
    group_len = left_piece.shape[0]
    seq_total = group_len * groups
    left_all, right_seq = (
        lax.all_gather(left_piece, "seq", axis=0, tiled=True),
        lax.all_gather(right_piece, "seq", axis=0, tiled=True),
    )
    right_all = gather_right(right_seq)
    offset = seq_index * own_rows
    summed = jnp.zeros((own_rows, columns, channels), jnp.float32)
    for group_id in range(groups):
        left_group = left_all[group_id * group_len : (group_id + 1) * group_len]
        row_slab = lax.dynamic_slice_in_dim(left_group, offset, own_rows, 2)
        right_group = right_all[group_id * group_len : (group_id + 1) * group_len]
        summed = summed + project_rows(row_slab, right_group, proj_weight)
    update = (summed / seq_total + proj_bias).astype(jnp.bfloat16)
    col_count = lax.axis_size("col")
    rowseq_count = lax.axis_size(("row", "seq"))
    run_len = own_rows // col_count
    section_one = move_cols(update.reshape(col_count, run_len, columns, channels))
    section_two = lax.all_to_all(
        section_one.reshape(run_len, rowseq_count, own_rows, channels),
        ("row", "seq"),
        split_axis=1,
        concat_axis=0,
        tiled=True,
    )
    section_three = move_cols(
        section_two.reshape(col_count, rowseq_count // col_count, 1, run_len, own_rows, channels)
    )
    mirrored = section_three.reshape(columns, own_rows, channels).transpose(1, 0, 2)
    middle = (
        pair_rep.astype(jnp.float32)
        + 0.5 * (update.astype(jnp.float32) + mirrored.astype(jnp.float32))
    ).astype(jnp.bfloat16)
    return transition(middle, norm_gain, up_weight, up_bias, down_weight, down_bias)


def solution(mesh):
    in_specs = (
        P("seq", None, "row"),
        P("seq", "row", "col"),
        P(),
        P(),
        P(("row", "seq"), "col", None),
        P(),
        P(),
        P(),
        P(),
        P(),
    )
    out_specs = P(("row", "seq"), "col", None)
    return jax.shard_map(
        on_device, mesh=mesh, in_specs=in_specs, out_specs=out_specs, check_vma=False
    )
```

profile of v0, /device:TPU:1, one launch (start us, length us, event | category | flops | bytes accessed | tf_op | source)
XLA Modules:
  0.0 234.8 jit_solution(6227691487281684803)
XLA Ops:
  7.3 15.7 %all_gather.10 = bf16[512,2,128]{2,1,0:T(2,128)(2,1)S(1)} all-gather(bf16[128,2,128]{2,1,0:T(2,128)(2,1)} %param.19), channel_id=1, replica_groups=mesh['row'=16,'col'=8,'seq'=4] {'seq'}, dimensions={0}, use_global_device_ids=true | all-gather | bytes 327680 | tf_op jit(solution)/shard_map/all_gather | solution.py:74
  23.8 43.0 %all-gather.3.cloned.1.call-done = bf16[512,32,64]{0,2,1:T(8,128)(2,1)} async-done(((bf16[128,32,64]{0,2,1:T(8,128)(2,1)}), bf16[512,32,64]{0,2,1:T(8,128)(2,1)}) %all-gather.3.cloned.1.call-update) | async-done | bytes 2097168 | tf_op jit(solution)/shard_map/all_gather | solution.py:73
  66.7 1.8 fusion.68
  69.9 46.1 %all-gather.5.cloned.1.call-done = bf16[512,32,128]{2,0,1:T(8,128)(2,1)} async-done(((bf16[512,2,128]{2,0,1:T(8,128)(2,1)}), bf16[512,32,128]{2,0,1:T(8,128)(2,1)}) %all-gather.5.cloned.1.call-update) | async-done | bytes 4194320 | tf_op jit(solution)/shard_map/all_gather | solution.py:46
  116.0 2.8 %fusion.67 = (bf16[128,32,128]{2,0,1:T(8,128)(2,1)S(1)}, bf16[128,32,128]{2,0,1:T(8,128)(2,1)S(1)}, bf16[128,32,128]{2,0,1:T(8,128)(2,1)S(1)}, bf16[128,32,128]{2,0,1:T(8,128)(2,1)S(1)}) fusion(bf16[512,32,128]{2,0,1:T(8,128)(2,1)} %all-gather.5.cloned.1.call-done), kind=kLoop, calls=%fused_computation.71 | loop fusion | bytes 8388608 | tf_op jit(solution)/shard_map/slice | solution.py:82
  120.9 1.7 copy.102
  122.6 1.1 broadcast.42.clone.2
  123.7 7.8 %while.40 = (s32[]{:T(128)}, f32[2,8,128,128]{3,2,1,0:T(8,128)}, bf16[2,128,32,8]{1,3,0,2:T(8,128)(2,1)}, bf16[128,32,128]{2,1,0:T(8,128)(2,1)}, bf16[1024,128]{1,0:T(8,128)(2,1)}, /*index=5*/s32[]{:T(128)}) while((s32[]{:T(128)}, f32[2,8,128,128]{3,2,1,0:T(8,128)}, bf16[2,128,32,8]{1,3,0,2:T(8,128)(2,1)}, bf16[128,32,128]{2,1,0:T(8,128)(2,1)}, ...), condition=%wide.region_1.2_spmd, body=%wide.region_0.1_spmd.sunk | while | flops 537919488 | bytes 15532201 | solution.py:28
  123.7 2.1 convolution_convert_fusion.8
  126.6 1.0 copy-done.2
  127.6 2.1 convolution_convert_fusion.8
  130.5 1.0 copy-done.2
  131.5 1.1 broadcast.42.clone.1
  132.5 6.9 %while.42 = (s32[]{:T(128)}, f32[2,8,128,128]{3,2,1,0:T(8,128)}, bf16[2,128,32,8]{1,3,0,2:T(8,128)(2,1)}, bf16[128,32,128]{2,1,0:T(8,128)(2,1)S(1)}, bf16[1024,128]{1,0:T(8,128)(2,1)}, /*index=5*/s32[]{:T(128)}) while((s32[]{:T(128)}, f32[2,8,128,128]{3,2,1,0:T(8,128)}, bf16[2,128,32,8]{1,3,0,2:T(8,128)(2,1)}, ...), condition=%wide.region_5.6_spmd, body=%wide.region_4.5_spmd.sunk | while | flops 537919488 | bytes 15532201 | solution.py:28
  132.5 1.7 convolution_convert_fusion.10
  136.0 1.7 convolution_convert_fusion.10
  139.6 3.5 %while.43 = (s32[]{:T(128)}, f32[2,8,128,128]{3,2,1,0:T(8,128)S(1)}, bf16[2,128,32,8]{1,3,0,2:T(8,128)(2,1)S(1)}, bf16[128,32,128]{2,1,0:T(8,128)(2,1)S(1)}, bf16[1024,128]{1,0:T(8,128)(2,1)}, /*index=5*/s32[]{:T(128)}) while((s32[]{:T(128)}, f32[2,8,128,128]{3,2,1,0:T(8,128)S(1)}, bf16[2,128,32,8]{1,3,0,2:T(8,128)(2,1)S(1)}, ...), condition=%wide.region_7.8_spmd, body=%wide.region_6.7_spmd.sunk | while | flops 537919488 | bytes 7143537 | solution.py:28
  144.1 3.6 %while.41 = (s32[]{:T(128)}, f32[2,8,128,128]{3,2,1,0:T(8,128)S(1)}, bf16[2,128,32,8]{1,3,0,2:T(8,128)(2,1)S(1)}, bf16[128,32,128]{2,1,0:T(8,128)(2,1)S(1)}, bf16[1024,128]{1,0:T(8,128)(2,1)}, /*index=5*/s32[]{:T(128)}) while((s32[]{:T(128)}, f32[2,8,128,128]{3,2,1,0:T(8,128)S(1)}, bf16[2,128,32,8]{1,3,0,2:T(8,128)(2,1)S(1)}, ...), condition=%wide.region_3.4_spmd, body=%wide.region_2.3_spmd.sunk | while | flops 537919488 | bytes 7143537 | solution.py:28
  147.7 1.8 add_multiply_fusion
  149.7 24.2 %all_to_all.39 = bf16[8,2,128,128]{3,2,1,0:T(8,128)(2,1)S(1)} all-to-all(bf16[8,2,128,128]{3,2,1,0:T(8,128)(2,1)S(1)} %add_convert_fusion), channel_id=1, replica_groups=mesh['row'=16,'col'=8,'seq'=4] {'col'}, dimensions={0} | all-to-all | bytes 1048576 | tf_op jit(solution)/shard_map/all_to_all | solution.py:50
  174.0 28.1 %all_to_all.40 = bf16[2,64,16,128]{3,2,0,1:T(8,128)(2,1)S(1)} all-to-all(bf16[2,64,16,128]{3,2,0,1:T(8,128)(2,1)S(1)} %copy.111), channel_id=1, replica_groups=mesh['row'=16,'col'=8,'seq'=4] {'row','seq'}, dimensions={1} | all-to-all | bytes 1048576 | tf_op jit(solution)/shard_map/all_to_all | solution.py:89
  202.1 20.6 %all_to_all.41 = bf16[8,8,1,2,16,128]{5,4,3,1,2,0:T(8,128)(2,1)S(1)} all-to-all(bf16[8,8,1,2,16,128]{5,4,3,1,2,0:T(8,128)(2,1)S(1)} %bitcast.205), channel_id=1, replica_groups=mesh['row'=16,'col'=8,'seq'=4] {'col'}, dimensions={0} | all-to-all | bytes 1048576 | tf_op jit(solution)/shard_map/all_to_all | solution.py:50
  222.8 1.0 fusion.60
  225.9 2.0 fusion.57
  (85 shorter events, 20.4 us)
Async XLA Ops:
  6.5 219.3 %copy-start = (bf16[512,128]{1,0:T(8,128)(2,1)S(1)}, bf16[512,128]{1,0:T(8,128)(2,1)}, u32[]{:S(2)}) copy-start(bf16[512,128]{1,0:T(8,128)(2,1)} %param.26) | copy-start | bytes 393220
  6.5 60.2 %all-gather.3.cloned.1.call-start = ((), (), s32[]{:S(2)}) async-start(), calls=%async_computation.3 | async-start | bytes 2621440 | tf_op jit(solution)/shard_map/all_gather | solution.py:73
  7.3 108.8 %all-gather.5.cloned.1.call-start = ((), (), s32[]{:S(2)}) async-start(), calls=%async_computation.4 | async-start | bytes 4456448 | tf_op jit(solution)/shard_map/all_gather | solution.py:46
  123.7 2.1 copy-start.1
  123.7 2.1 copy-start.10
  126.6 1.0 copy-start.2
  127.6 2.1 copy-start.1
  127.6 2.1 copy-start.10
  130.5 1.0 copy-start.2
  132.5 1.7 copy-start.4
  132.5 1.7 copy-start.11
  135.0 1.0 copy-start.5
  136.0 1.7 copy-start.4
  136.0 1.7 copy-start.11
  138.5 1.0 copy-start.5
  143.1 1.0 copy-start.6
  144.1 3.6 %copy-start.3 = (f32[2,8,128,128]{3,2,1,0:T(8,128)S(1)}, f32[2,8,128,128]{3,2,1,0:T(8,128)}, u32[]{:S(2)}) copy-start(f32[2,8,128,128]{3,2,1,0:T(8,128)} %get-tuple-element.113) | copy-start | bytes 3145732
  144.1 1.0 copy-start.13
  147.7 1.9 copy-start.8
  174.0 48.8 %copy-start.7 = (bf16[16,128,128]{2,1,0:T(8,128)(2,1)S(1)}, bf16[16,128,128]{2,1,0:T(8,128)(2,1)}, u32[]{:S(2)}) copy-start(bf16[16,128,128]{2,1,0:T(8,128)(2,1)} %param.22) | copy-start | bytes 1572868
  223.8 1.4 copy-start.9
  224.2 1.7 copy-start.14
  224.2 1.7 copy-start.15
  224.2 1.7 copy-start.16
  (3 other events, 2.9 us)
Sparse Core Ops, SparseCore 0:
  9.4 57.2 all-gather.2
  68.9 47.1 all-gather.4
where the time goes:
time: 235 us
  waiting for transfers between devices  89.8 us (38%)
  blocking collectives  88.6 us (38%)
  local copies, waits for them, and re-layouts  18.9 us (8%)
  matrix products  18.8 us (8%)
  between operations  13.7 us (6%)
  other arithmetic  4.69 us (2%)
    all_gather x1, waiting for transfers between devices, gather_right(): return lax.all_gather(right_part, 'row', axis=1, tiled=True)  46.1 us
    all_to_all x2, blocking collectives, move_cols(): return lax.all_to_all(tile, 'col', split_axis=0, concat_axis=2, tiled=True)  44.8 us
    all_gather x1, waiting for transfers between devices, on_device(): lax.all_gather(left_piece, 'seq', axis=0, tiled=True)  43 us
    all_to_all x1, blocking collectives, on_device(): lax.all_to_all(section_one.reshape(run_len, rowseq_count, own_rows, chann...  28.1 us
    all_gather x1, blocking collectives, on_device(): lax.all_gather(right_piece, 'seq', axis=0, tiled=True)  15.7 us
    dot_general x8, matrix products, project_block(): lax.dot_general(left_mat, right_mat, (((0,), (0,)), ((), ())), preferred_...  10.5 us
    dot_general x8, matrix products, project_block(): jnp.dot(outer_prod, proj_weight, preferred_element_type=jnp.float32)  6.24 us
    while x32, local copies, waits for them, and re-layouts  4.73 us
  transfers between devices with their start and end apart: 2, of which 2 were waited for; matrix products, arithmetic and copies ran while one was open for 2% of the time, Pallas kernels for 0%

commit v1 on v0

--- a/solution.py
+++ b/solution.py
@@ -1,9 +1,26 @@
+import functools
 import jax
 import jax.numpy as jnp
 from jax import lax
 from jax.sharding import PartitionSpec as P
 
 epsilon = 1e-05
+
+
+def _show_row(body, a_name):
+    x_now = jnp.concatenate(
+        lax.all_to_all(
+            jnp.stack(jnp.split(body, lax.axis_size(a_name), axis=0), axis=0),
+            a_name,
+            split_axis=0,
+            concat_axis=0,
+        ),
+        axis=2,
+    )
+    return x_now
+
+
+connect_tails = functools.partial(_show_row, a_name="col")
 
 
 def project_block(row_slab, right_all, proj_weight):
@@ -47,7 +64,7 @@
 
 
 def move_cols(tile):
-    return lax.all_to_all(tile, "col", split_axis=0, concat_axis=2, tiled=True)
+    return connect_tails(tile)
 
 
 def on_device(

time: 235 us -> 236 us (level)
  no operation moved by 1% of the time
where the time goes in v1:
time: 236 us
  waiting for transfers between devices  89.9 us (38%)
  blocking collectives  88.4 us (37%)
  local copies, waits for them, and re-layouts  19.7 us (8%)
  matrix products  18.8 us (8%)
  between operations  13.7 us (6%)
  other arithmetic  5.18 us (2%)
    all_gather x1, waiting for transfers between devices, gather_right(): return lax.all_gather(right_part, 'row', axis=1, tiled=True)  46.2 us
    all_to_all x2, blocking collectives, _show_row(): lax.all_to_all(jnp.stack(jnp.split(body, lax.axis_size(a_name), axis=0),...  44.8 us
    all_gather x1, waiting for transfers between devices, on_device(): lax.all_gather(left_piece, 'seq', axis=0, tiled=True)  43 us
    all_to_all x1, blocking collectives, on_device(): lax.all_to_all(section_one.reshape(run_len, rowseq_count, own_rows, chann...  28 us
    all_gather x1, blocking collectives, on_device(): lax.all_gather(right_piece, 'seq', axis=0, tiled=True)  15.7 us
    dot_general x8, matrix products, project_block(): lax.dot_general(left_mat, right_mat, (((0,), (0,)), ((), ())), preferred_...  10.5 us
    dot_general x8, matrix products, project_block(): jnp.dot(outer_prod, proj_weight, preferred_element_type=jnp.float32)  6.24 us
    while x32, local copies, waits for them, and re-layouts  4.73 us
  transfers between devices with their start and end apart: 2, of which 2 were waited for; matrix products, arithmetic and copies ran while one was open for 2% of the time, Pallas kernels for 0%

profile of v1, /device:TPU:1, one launch (start us, length us, event | category | flops | bytes accessed | tf_op | source)
XLA Modules:
  0.0 236.0 jit_solution(3697710945286846450)
XLA Ops:
  7.3 15.7 %all_gather.10 = bf16[512,2,128]{2,1,0:T(2,128)(2,1)S(1)} all-gather(bf16[128,2,128]{2,1,0:T(2,128)(2,1)} %param.19), channel_id=1, replica_groups=mesh['row'=16,'col'=8,'seq'=4] {'seq'}, dimensions={0}, use_global_device_ids=true | all-gather | bytes 327680 | tf_op jit(solution)/shard_map/all_gather | solution.py:91
  23.8 43.0 %all-gather.3.cloned.1.call-done = bf16[512,32,64]{0,2,1:T(8,128)(2,1)} async-done(((bf16[128,32,64]{0,2,1:T(8,128)(2,1)}), bf16[512,32,64]{0,2,1:T(8,128)(2,1)}) %all-gather.3.cloned.1.call-update) | async-done | bytes 2097168 | tf_op jit(solution)/shard_map/all_gather | solution.py:90
  66.7 1.7 fusion.84
  69.9 46.2 %all-gather.5.cloned.1.call-done = bf16[512,32,128]{2,0,1:T(8,128)(2,1)} async-done(((bf16[512,2,128]{2,0,1:T(8,128)(2,1)}), bf16[512,32,128]{2,0,1:T(8,128)(2,1)}) %all-gather.5.cloned.1.call-update) | async-done | bytes 4194320 | tf_op jit(solution)/shard_map/all_gather | solution.py:63
  116.0 2.8 %fusion.83 = (bf16[128,32,128]{2,0,1:T(8,128)(2,1)S(1)}, bf16[128,32,128]{2,0,1:T(8,128)(2,1)S(1)}, bf16[128,32,128]{2,0,1:T(8,128)(2,1)S(1)}, bf16[128,32,128]{2,0,1:T(8,128)(2,1)S(1)}) fusion(bf16[512,32,128]{2,0,1:T(8,128)(2,1)} %all-gather.5.cloned.1.call-done), kind=kLoop, calls=%fused_computation.102 | loop fusion | bytes 8388608 | tf_op jit(solution)/shard_map/slice | solution.py:99
  120.9 1.7 copy.160
  122.6 1.1 broadcast.38.clone.2
  123.7 7.8 %while.40 = (s32[]{:T(128)}, f32[2,8,128,128]{3,2,1,0:T(8,128)}, bf16[2,128,32,8]{1,3,0,2:T(8,128)(2,1)}, bf16[128,32,128]{2,1,0:T(8,128)(2,1)}, bf16[1024,128]{1,0:T(8,128)(2,1)}, /*index=5*/s32[]{:T(128)}) while((s32[]{:T(128)}, f32[2,8,128,128]{3,2,1,0:T(8,128)}, bf16[2,128,32,8]{1,3,0,2:T(8,128)(2,1)}, bf16[128,32,128]{2,1,0:T(8,128)(2,1)}, ...), condition=%wide.region_1.2_spmd, body=%wide.region_0.1_spmd.sunk | while | flops 537919488 | bytes 15532201 | solution.py:45
  123.7 2.1 convolution_convert_fusion.8
  126.6 1.0 copy-done.2
  127.6 2.1 convolution_convert_fusion.8
  130.5 1.0 copy-done.2
  131.5 1.1 broadcast.38.clone.1
  132.5 6.9 %while.42 = (s32[]{:T(128)}, f32[2,8,128,128]{3,2,1,0:T(8,128)}, bf16[2,128,32,8]{1,3,0,2:T(8,128)(2,1)}, bf16[128,32,128]{2,1,0:T(8,128)(2,1)S(1)}, bf16[1024,128]{1,0:T(8,128)(2,1)}, /*index=5*/s32[]{:T(128)}) while((s32[]{:T(128)}, f32[2,8,128,128]{3,2,1,0:T(8,128)}, bf16[2,128,32,8]{1,3,0,2:T(8,128)(2,1)}, ...), condition=%wide.region_5.6_spmd, body=%wide.region_4.5_spmd.sunk | while | flops 537919488 | bytes 15532201 | solution.py:45
  132.5 1.7 convolution_convert_fusion.10
  136.0 1.7 convolution_convert_fusion.10
  139.6 3.5 %while.43 = (s32[]{:T(128)}, f32[2,8,128,128]{3,2,1,0:T(8,128)S(1)}, bf16[2,128,32,8]{1,3,0,2:T(8,128)(2,1)S(1)}, bf16[128,32,128]{2,1,0:T(8,128)(2,1)S(1)}, bf16[1024,128]{1,0:T(8,128)(2,1)}, /*index=5*/s32[]{:T(128)}) while((s32[]{:T(128)}, f32[2,8,128,128]{3,2,1,0:T(8,128)S(1)}, bf16[2,128,32,8]{1,3,0,2:T(8,128)(2,1)S(1)}, ...), condition=%wide.region_7.8_spmd, body=%wide.region_6.7_spmd.sunk | while | flops 537919488 | bytes 7143537 | solution.py:45
  144.1 3.6 %while.41 = (s32[]{:T(128)}, f32[2,8,128,128]{3,2,1,0:T(8,128)S(1)}, bf16[2,128,32,8]{1,3,0,2:T(8,128)(2,1)S(1)}, bf16[128,32,128]{2,1,0:T(8,128)(2,1)S(1)}, bf16[1024,128]{1,0:T(8,128)(2,1)}, /*index=5*/s32[]{:T(128)}) while((s32[]{:T(128)}, f32[2,8,128,128]{3,2,1,0:T(8,128)S(1)}, bf16[2,128,32,8]{1,3,0,2:T(8,128)(2,1)S(1)}, ...), condition=%wide.region_3.4_spmd, body=%wide.region_2.3_spmd.sunk | while | flops 537919488 | bytes 7143537 | solution.py:45
  147.7 1.8 add_multiply_fusion
  151.0 24.2 %all_to_all.25 = bf16[8,1,2,128,128]{4,3,2,1,0:T(8,128)(2,1)S(1)} all-to-all(bf16[8,1,2,128,128]{4,3,2,1,0:T(8,128)(2,1)S(1)} %copy.168), channel_id=1, replica_groups=mesh['row'=16,'col'=8,'seq'=4] {'col'}, dimensions={0} | all-to-all | bytes 1048576 | tf_op jit(solution)/shard_map/all_to_all | solution.py:12
  175.3 28.0 %all_to_all.26 = bf16[2,64,16,128]{3,2,0,1:T(8,128)(2,1)S(1)} all-to-all(bf16[2,64,16,128]{3,2,0,1:T(8,128)(2,1)S(1)} %copy.170), channel_id=1, replica_groups=mesh['row'=16,'col'=8,'seq'=4] {'row','seq'}, dimensions={1} | all-to-all | bytes 1048576 | tf_op jit(solution)/shard_map/all_to_all | solution.py:106
  203.4 20.5 %all_to_all.27 = bf16[8,1,8,1,2,16,128]{6,5,4,2,3,1,0:T(8,128)(2,1)S(1)} all-to-all(bf16[8,1,8,1,2,16,128]{6,5,4,2,3,1,0:T(8,128)(2,1)S(1)} %fusion.65), channel_id=1, replica_groups=mesh['row'=16,'col'=8,'seq'=4] {'col'}, dimensions={0} | all-to-all | bytes 1048576 | tf_op jit(solution)/shard_map/all_to_all | solution.py:12
  224.1 1.0 fusion.60
  227.1 2.0 fusion.57
  (102 shorter events, 21.8 us)
Async XLA Ops:
  6.5 220.6 %copy-start = (bf16[512,128]{1,0:T(8,128)(2,1)S(1)}, bf16[512,128]{1,0:T(8,128)(2,1)}, u32[]{:S(2)}) copy-start(bf16[512,128]{1,0:T(8,128)(2,1)} %param.26) | copy-start | bytes 393220
  6.5 60.2 %all-gather.3.cloned.1.call-start = ((), (), s32[]{:S(2)}) async-start(), calls=%async_computation.3 | async-start | bytes 2621440 | tf_op jit(solution)/shard_map/all_gather | solution.py:90
  7.3 108.8 %all-gather.5.cloned.1.call-start = ((), (), s32[]{:S(2)}) async-start(), calls=%async_computation.4 | async-start | bytes 4456448 | tf_op jit(solution)/shard_map/all_gather | solution.py:63
  123.7 2.1 copy-start.1
  123.7 2.1 copy-start.10
  126.6 1.0 copy-start.2
  127.6 2.1 copy-start.1
  127.6 2.1 copy-start.10
  130.5 1.0 copy-start.2
  132.5 1.7 copy-start.4
  132.5 1.7 copy-start.11
  135.0 1.0 copy-start.5
  136.0 1.7 copy-start.4
  136.0 1.7 copy-start.11
  138.5 1.0 copy-start.5
  143.1 1.0 copy-start.6
  144.1 3.6 %copy-start.3 = (f32[2,8,128,128]{3,2,1,0:T(8,128)S(1)}, f32[2,8,128,128]{3,2,1,0:T(8,128)}, u32[]{:S(2)}) copy-start(f32[2,8,128,128]{3,2,1,0:T(8,128)} %get-tuple-element.113) | copy-start | bytes 3145732
  144.1 1.0 copy-start.13
  147.7 1.9 copy-start.8
  203.2 20.8 %copy-start.7 = (bf16[16,128,128]{2,1,0:T(8,128)(2,1)S(1)}, bf16[16,128,128]{2,1,0:T(8,128)(2,1)}, u32[]{:S(2)}) copy-start(bf16[16,128,128]{2,1,0:T(8,128)(2,1)} %param.22) | copy-start | bytes 1572868
  225.1 1.4 copy-start.9
  225.4 1.7 copy-start.14
  225.4 1.7 copy-start.15
  225.5 1.7 copy-start.16
  (3 other events, 2.9 us)
Sparse Core Ops, SparseCore 0:
  9.4 57.2 all-gather.2
  68.9 47.1 all-gather.4
